TPU v7x, 32 devices: a whole 2x2x4 slice. The times are simulated.
32 devices in a mesh: dp: 2 (over core), ep: 16 (over z, y, x).
Axes of the slice: x: 2, y: 2, z: 4, core: 2. Of those that a mesh axis runs over, the one named last changes fastest.
Arguments:
- latent_cache: bfloat16 [16, 4, 512, 576], P('ep', 'dp'), may hold values from -6 to 6
- lengths: int32 [16, 4], P(None, 'dp'), may hold values from 2 to 512
- new_home: int32 [16, 4], P(None, 'dp'), may hold values from 0 to 15, as said below
- queries: bfloat16 [2, 16, 4, 128, 576], P(None, 'ep', 'dp'), may hold values from -32 to 32
- new_latent: bfloat16 [2, 16, 4, 576], P(None, 'ep', 'dp'), may hold values from -6 to 6
- hidden: bfloat16 [2, 16, 4, 3584], P(None, 'ep', 'dp'), may hold values from -6 to 6
- routes: int32 [2, 16, 4, 8], P(None, 'ep', 'dp'), may hold values from 0 to 15, all different within a row; in each aligned block of 4 rows (0 to 3, 4 to 7, ..., all dimensions but the last counted through in order) at most 4 rows name the same one
- route_logits: bfloat16 [2, 16, 4, 8], P(None, 'ep', 'dp'), may hold values from -8 to 8
- w_gate: bfloat16 [16, 3584, 1024], P('ep', None, 'dp'), may hold values from -0.09375 to 0.09375
- w_up: bfloat16 [16, 3584, 1024], P('ep', None, 'dp'), may hold values from -0.09375 to 0.09375
- w_down: bfloat16 [16, 1024, 3584], P('ep', 'dp'), may hold values from -0.1875 to 0.1875
Outputs:
- attended: bfloat16 [2, 16, 4, 128, 512], P(None, 'ep', 'dp')
- moe_out: bfloat16 [2, 16, 4, 3584], P(None, 'ep', 'dp')
Inputs may be any that keep to these rules, and one draw needn't show every extreme that they name: `routes`: in each step, the 4 requests of one ep index name any one expert in at most 4 of their choices, and this bound is reached. For each request index c, new_home[., c] exchanges exactly two ep indices and leaves every other one in place, so new_home[new_home[e, c], c] == e; the two indices lie 16 // 2 apart for even c and 1 apart (modulo 16) for odd c.
All inputs are finite; a program needn't handle non-finite values.
Results may differ from a plain program's by a relative error of at most 0.0057.
Values may be sent and summed in bfloat16 or wider, within the bound.
A program may use at most 128 MiB of HBM per device.

v0:
```python
import math
import jax
import jax.numpy as jnp
from jax import lax
from jax.sharding import PartitionSpec as P

KV_RANK = 512
HEAD_QK = 192


def spread(value, axis, source):
    kept = jnp.where(lax.axis_index(axis) == source, value, 0).astype(value.dtype)
    return lax.psum(kept, axis)


def attend(query_rows, cache_rows, fresh_rows, length, softmax_scale):
    step_count, head_count, lat_width = query_rows.shape
    flat_query = query_rows.reshape(step_count * head_count, lat_width)
    total_keys = cache_rows.shape[0]
    key_block = math.gcd(128, total_keys)
    block_count = (length + key_block - 1) // key_block

    def score_block(block_index, buffer):
        key_rows = lax.dynamic_slice_in_dim(cache_rows, block_index * key_block, key_block, 0)
        block_scores = (
            jnp.dot(flat_query, key_rows.T, preferred_element_type=jnp.float32) * softmax_scale
        )
        key_place = block_index * key_block + jnp.arange(key_block, dtype=jnp.int32)
        block_scores = jnp.where(key_place[None, :] < length, block_scores, -jnp.inf)
        return lax.dynamic_update_slice_in_dim(buffer, block_scores, block_index * key_block, 1)

    empty_scores = jnp.full((step_count * head_count, total_keys), -jnp.inf, jnp.float32)
    cache_scores = lax.fori_loop(0, block_count, score_block, empty_scores)
    fresh_scores = (
        jnp.dot(flat_query, fresh_rows.T, preferred_element_type=jnp.float32) * softmax_scale
    )
    row_step = jnp.arange(step_count * head_count, dtype=jnp.int32) // head_count
    fresh_step = jnp.arange(step_count, dtype=jnp.int32)
    fresh_scores = jnp.where(fresh_step[None, :] <= row_step[:, None], fresh_scores, -jnp.inf)
    row_max = jnp.maximum(jnp.max(cache_scores, 1), jnp.max(fresh_scores, 1))[:, None]
    cache_weights = jnp.exp(cache_scores - row_max)
    fresh_weights = jnp.exp(fresh_scores - row_max)
    row_total = jnp.sum(cache_weights, 1, keepdims=True) + jnp.sum(fresh_weights, 1, keepdims=True)
    cache_probs = (cache_weights / row_total).astype(jnp.bfloat16)
    fresh_probs = (fresh_weights / row_total).astype(jnp.bfloat16)

    def value_block(block_index, value_sum):
        key_rows = lax.dynamic_slice_in_dim(cache_rows, block_index * key_block, key_block, 0)
        prob_block = lax.dynamic_slice_in_dim(cache_probs, block_index * key_block, key_block, 1)
        return value_sum + jnp.dot(
            prob_block, key_rows[:, :KV_RANK], preferred_element_type=jnp.float32
        )

    start_sum = jnp.dot(fresh_probs, fresh_rows[:, :KV_RANK], preferred_element_type=jnp.float32)
    value_sum = lax.fori_loop(0, block_count, value_block, start_sum)
    return value_sum.astype(jnp.bfloat16).reshape(step_count, head_count, KV_RANK)


def shards(
    latent_cache,
    lengths,
    new_home,
    queries,
    new_latent,
    hidden,
    routes,
    route_logits,
    w_gate,
    w_up,
    w_down,
):
    expert_count = lax.axis_size("ep")
    own_rank = lax.axis_index("ep")
    rank_ids = jnp.arange(expert_count, dtype=jnp.int32)
    softmax_scale = HEAD_QK ** (-0.5)
    step_count = queries.shape[0]
    attended_rows = []
    for request in range(latent_cache.shape[1]):
        home_ranks = new_home[:, request]
        anchor = home_ranks[own_rank]
        first_sender = jnp.argmax(home_ranks != rank_ids)
        second_sender = home_ranks[first_sender]
        own_cache = latent_cache[0, request]
        own_query = queries[:, 0, request]
        own_fresh = new_latent[:, 0, request]
        computed = attend(
            own_query, own_cache, own_fresh, lengths[own_rank, request], softmax_scale
        )
        result = computed
        for sender in (first_sender, second_sender):
            arrived = spread(computed, "ep", sender)
            result = jnp.where((anchor == sender) & (anchor != own_rank), arrived, result)
        attended_rows.append(result)
    attended = jnp.stack(attended_rows, 1)[:, None]
    gathered = (
        lax.all_gather(hidden[:, 0], "dp", axis=1, tiled=True),
        lax.all_gather(routes[:, 0], "dp", axis=1, tiled=True),
        lax.all_gather(route_logits[:, 0], "dp", axis=1, tiled=True),
    )
    col_hidden, col_routes, col_logits = gathered
    column_rows = col_hidden.shape[1]
    top_count = routes.shape[3]
    model_width = hidden.shape[3]
    capacity = max(2, 2 * column_rows * top_count // expert_count)
    sigmoid_part = jax.nn.sigmoid(col_logits.astype(jnp.float32))
    gate_weights = 2.5 * sigmoid_part / jnp.sum(sigmoid_part, -1, keepdims=True)
    slot_ids = jnp.arange(expert_count * capacity, dtype=jnp.int32)

    def dispatch_plan(step_routes):
        flat_routes = step_routes.reshape(-1)
        onehot = (flat_routes[:, None] == rank_ids[None, :]).astype(jnp.int32)
        earlier = jnp.sum(jnp.cumsum(onehot, 0) * onehot, 1) - 1
        return flat_routes * capacity + earlier

    def build_buffer(step_hidden, placed):
        chosen = placed.reshape(column_rows, top_count)[None, :, :] == slot_ids[:, None, None]
        selector = jnp.any(chosen, 2).astype(jnp.bfloat16)
        filled = jnp.dot(selector, step_hidden, preferred_element_type=jnp.float32).astype(
            jnp.bfloat16
        )
        return filled.reshape(expert_count, capacity, model_width)

    def expert_math(received):
        source_count, item_count, _ = received.shape
        flat_rows = received.reshape(source_count * item_count, model_width)
        gate_part = jnp.dot(flat_rows, w_gate[0], preferred_element_type=jnp.float32)
        up_part = jnp.dot(flat_rows, w_up[0], preferred_element_type=jnp.float32)
        hidden_units = (jax.nn.silu(gate_part) * up_part).astype(jnp.bfloat16)
        partial_value = jnp.dot(hidden_units, w_down[0], preferred_element_type=jnp.float32).astype(
            jnp.bfloat16
        )
        return partial_value.reshape(source_count, item_count, model_width)

    def expert_apart(received):
        return lax.all_to_all(expert_math(received), "ep", split_axis=0, concat_axis=0, tiled=True)

    def combine(returned, placed, step_gates):
        flat_out = returned.reshape(expert_count * capacity, model_width)
        picked = jnp.take(flat_out, placed, axis=0).astype(jnp.float32)
        weighted = picked * step_gates.reshape(-1)[:, None]
        return jnp.sum(weighted.reshape(column_rows, top_count, model_width), 1)

    placements = [dispatch_plan(col_routes[number]) for number in range(step_count)]
    buffers = [build_buffer(col_hidden[number], placements[number]) for number in range(step_count)]
    returned_list = [
        expert_apart(lax.all_to_all(buffers[number], "ep", split_axis=0, concat_axis=0, tiled=True))
        for number in range(step_count)
    ]
    partials = jnp.stack(
        [
            combine(returned_list[number], placements[number], gate_weights[number])
            for number in range(step_count)
        ],
        0,
    )
    summed = lax.psum_scatter(partials, "dp", scatter_dimension=1, tiled=True)
    moe_out = summed.astype(jnp.bfloat16)[:, None]
    return (attended, moe_out)


def solution(mesh):
    placed = (
        P("ep", "dp", None, None),
        P(None, "dp"),
        P(None, "dp"),
        P(None, "ep", "dp", None, None),
        P(None, "ep", "dp", None),
        P(None, "ep", "dp", None),
        P(None, "ep", "dp", None),
        P(None, "ep", "dp", None),
        P("ep", None, "dp"),
        P("ep", None, "dp"),
        P("ep", "dp", None),
    )
    return jax.shard_map(
        shards,
        mesh=mesh,
        in_specs=placed,
        out_specs=(P(None, "ep", "dp", None, None), P(None, "ep", "dp", None)),
        check_vma=False,
    )
```

profile of v0, /device:TPU:0, one launch (start us, length us, event | category | flops | bytes accessed | tf_op | source)
XLA Modules:
  0.0 191.3 jit_solution(3648106268967699894)
XLA Ops:
  7.9 2.0 %all-gather = s32[2,1,4,8]{3,0,1,2:T(2,128)S(1)} all-gather(s32[2,1,2,8]{3,0,1,2:T(2,128)S(1)} %copy.84), channel_id=2, replica_groups=mesh['dp'=2,'ep'=16] {'dp'}, dimensions={2}, use_global_device_ids=true | all-gather | bytes 384 | tf_op jit(solution)/shard_map/all_gather | solution.py:97
  10.5 0.8 copy.85
  11.3 1.8 all-gather.1
  13.6 0.9 reshape.131
  14.5 8.2 %all-to-all-start = ((bf16[16,4,3584]{2,1,0:T(4,128)(2,1)}), bf16[16,4,3584]{2,1,0:T(4,128)(2,1)}, u32[]{:S(2)}, u32[]{:S(2)}) async-start(bf16[16,4,3584]{2,1,0:T(4,128)(2,1)} %reshape.131), calls=%async_computation | async-start | bytes 917504 | tf_op jit(solution)/shard_map/all_to_all | solution.py:146
  22.8 1.4 compare_reduce_fusion
  25.4 0.8 fusion.85
  26.8 1.4 constant_dynamic-slice_fusion.1
  28.9 1.3 fusion.80
  30.5 0.8 fusion.81
  31.6 0.9 while.40
  37.2 1.2 copy.80
  38.4 1.0 while.42
  45.7 0.8 broadcast_select_fusion.2
  46.5 0.8 broadcast_select_fusion
  47.4 1.8 all-gather.2
  50.2 0.9 reshape.136
  51.2 11.6 %all-to-all-start.2 = ((bf16[16,4,3584]{2,1,0:T(4,128)(2,1)}), bf16[16,4,3584]{2,1,0:T(4,128)(2,1)S(1)}, u32[]{:S(2)}, u32[]{:S(2)}) async-start(bf16[16,4,3584]{2,1,0:T(4,128)(2,1)} %reshape.136), calls=%async_computation.2 | async-start | bytes 917504 | tf_op jit(solution)/shard_map/all_to_all | solution.py:146
  62.9 1.1 reshape.132
  64.0 2.8 %fusion.24 = f32[64,512]{1,0:T(8,128)S(1)} fusion(bf16[64,3584]{1,0:T(8,128)(2,1)S(1)} %reshape.132, bf16[1,3584,512]{2,1,0:T(8,128)(2,1)} %param.29), kind=kOutput, calls=%fused_computation.36 | convolution fusion | flops 234881024 | bytes 4259840 | tf_op jit(solution)/shard_map/dot_general | solution.py:126
  66.8 4.7 %convolution_convert_fusion.1 = bf16[64,3584]{1,0:T(8,128)(2,1)S(1)} fusion(bf16[1,512,3584]{2,1,0:T(8,128)(2,1)} %param.31, bf16[64,3584]{1,0:T(8,128)(2,1)S(1)} %reshape.132, bf16[1,3584,512]{2,1,0:T(8,128)(2,1)} %param.30, f32[64,512]{1,0:T(8,128)S(1)} %fusion.24), kind=kOutput, calls=%fused_computation.25 | convolution fusion | flops 470188032 | bytes 8388608 | tf_op jit(solution)/shard_map/dot_general | solution.py:129
  71.5 0.9 reshape.133
  72.4 9.0 %all-to-all-done.2 = bf16[16,4,3584]{2,1,0:T(4,128)(2,1)S(1)} async-done(((bf16[16,4,3584]{2,1,0:T(4,128)(2,1)}), bf16[16,4,3584]{2,1,0:T(4,128)(2,1)S(1)}, u32[]{:S(2)}, u32[]{:S(2)}) %all-to-all-start.2) | async-done | bytes 458784 | tf_op jit(solution)/shard_map/all_to_all | solution.py:146
  81.4 4.8 %all-to-all-start.1 = ((bf16[16,4,3584]{2,1,0:T(4,128)(2,1)}), bf16[16,4,3584]{2,1,0:T(4,128)(2,1)S(1)}, u32[]{:S(2)}, u32[]{:S(2)}) async-start(bf16[16,4,3584]{2,1,0:T(4,128)(2,1)} %reshape.133), calls=%async_computation.1 | async-start | bytes 917504 | tf_op jit(solution)/shard_map/all_to_all | solution.py:135
  86.3 2.8 %fusion.22 = f32[64,512]{1,0:T(8,128)S(1)} fusion(bf16[64,3584]{1,0:T(8,128)(2,1)S(1)} %reshape.137, bf16[1,3584,512]{2,1,0:T(8,128)(2,1)} %param.29), kind=kOutput, calls=%fused_computation.34 | convolution fusion | flops 234881024 | bytes 4259840 | tf_op jit(solution)/shard_map/dot_general | solution.py:126
  89.1 4.6 %convolution_convert_fusion = bf16[64,3584]{1,0:T(8,128)(2,1)S(1)} fusion(bf16[1,512,3584]{2,1,0:T(8,128)(2,1)} %param.31, bf16[64,3584]{1,0:T(8,128)(2,1)S(1)} %reshape.137, bf16[1,3584,512]{2,1,0:T(8,128)(2,1)} %param.30, f32[64,512]{1,0:T(8,128)S(1)} %fusion.22), kind=kOutput, calls=%fused_computation.24 | convolution fusion | flops 470188032 | bytes 8388608 | tf_op jit(solution)/shard_map/dot_general | solution.py:129
  93.8 0.9 reshape.138
  94.6 6.5 %all-to-all-done.1 = bf16[16,4,3584]{2,1,0:T(4,128)(2,1)S(1)} async-done(((bf16[16,4,3584]{2,1,0:T(4,128)(2,1)}), bf16[16,4,3584]{2,1,0:T(4,128)(2,1)S(1)}, u32[]{:S(2)}, u32[]{:S(2)}) %all-to-all-start.1) | async-done | bytes 458784 | tf_op jit(solution)/shard_map/all_to_all | solution.py:135
  101.1 3.7 %all-to-all-start.3 = ((bf16[16,4,3584]{2,1,0:T(4,128)(2,1)}), bf16[16,4,3584]{2,1,0:T(4,128)(2,1)S(1)}, u32[]{:S(2)}, u32[]{:S(2)}) async-start(bf16[16,4,3584]{2,1,0:T(4,128)(2,1)} %reshape.138), calls=%async_computation.3 | async-start | bytes 917504 | tf_op jit(solution)/shard_map/all_to_all | solution.py:135
  112.6 64.3 %all-reduce.4.cloned.1.call-done = (bf16[2,128,512]{2,1,0:T(8,128)(2,1)}, bf16[2,128,512]{2,1,0:T(8,128)(2,1)}, bf16[2,128,512]{2,1,0:T(8,128)(2,1)}, bf16[2,128,512]{2,1,0:T(8,128)(2,1)}) async-done(((bf16[2,128,512]{2,1,0:T(8,128)(2,1)}, bf16[2,128,512]{2,1,0:T(8,128)(2,1)}, bf16[2,128,512]{2,1,0:T(8,128)(2,1)}, bf16[2,128,512]{2,1,0:T(8,128)(2,1)}), (bf16[2,128,512]{2,1,0:T(8,128)(2,1)}, ...) | async-done | bytes 1048592 | tf_op jit(solution)/shard_map/psum | solution.py:13
  177.0 0.8 maximum_bitcast_fusion
  180.0 3.8 %all-reduce = bf16[2,4,3584]{2,1,0:T(4,128)(2,1)S(1)} all-reduce(f32[2,4,3584]{2,1,0:T(4,128)S(1)} %pad_maximum_fusion), channel_id=5, replica_groups=mesh['dp'=2,'ep'=16] {'dp'}, use_global_device_ids=true, to_apply=%region_31.33.clone | all-reduce | flops 28672 | bytes 172032
  (99 shorter events, 15.5 us)
Async XLA Ops:
  7.2 23.3 %copy-start = (bf16[2,1,2,128,576]{3,4,2,1,0:T(8,128)(2,1)S(1)}, bf16[2,1,2,128,576]{3,4,2,1,0:T(8,128)(2,1)}, u32[]{:S(2)}) copy-start(bf16[2,1,2,128,576]{3,4,2,1,0:T(8,128)(2,1)} %param.24) | copy-start | bytes 1769476
  10.3 1.0 copy-start.2
  14.5 36.7 %all-to-all-start = ((bf16[16,4,3584]{2,1,0:T(4,128)(2,1)}), bf16[16,4,3584]{2,1,0:T(4,128)(2,1)}, u32[]{:S(2)}, u32[]{:S(2)}) async-start(bf16[16,4,3584]{2,1,0:T(4,128)(2,1)} %reshape.131), calls=%async_computation | async-start | bytes 917504 | tf_op jit(solution)/shard_map/all_to_all | solution.py:146
  22.7 154.2 %all-reduce.4.cloned.1.call-start = ((), (), s32[]{:S(2)}) async-start(), calls=%async_computation.4 | async-start | bytes 2097152 | tf_op jit(solution)/shard_map/psum | solution.py:13
  30.5 2.3 %copy-start.1 = (bf16[2,1,2,576]{3,2,1,0:T(2,128)(2,1)S(1)}, bf16[2,1,2,576]{3,2,1,0:T(2,128)(2,1)}, u32[]{:S(2)}) copy-start(bf16[2,1,2,576]{3,2,1,0:T(2,128)(2,1)} %param.25) | copy-start | bytes 13828
  31.6 2.3 %copy-start.4 = (s32[16,2]{0,1:T(2,128)S(1)}, s32[16,2]{0,1:T(2,128)}, u32[]{:S(2)}) copy-start(s32[16,2]{0,1:T(2,128)} %param.23) | copy-start | bytes 388
  42.9 2.8 %copy-start.5 = (bf16[2,1,2,8]{3,2,1,0:T(2,128)(2,1)S(1)}, bf16[2,1,2,8]{3,2,1,0:T(2,128)(2,1)}, u32[]{:S(2)}) copy-start(bf16[2,1,2,8]{3,2,1,0:T(2,128)(2,1)} %param.28) | copy-start | bytes 196
  51.2 30.2 %all-to-all-start.2 = ((bf16[16,4,3584]{2,1,0:T(4,128)(2,1)}), bf16[16,4,3584]{2,1,0:T(4,128)(2,1)S(1)}, u32[]{:S(2)}, u32[]{:S(2)}) async-start(bf16[16,4,3584]{2,1,0:T(4,128)(2,1)} %reshape.136), calls=%async_computation.2 | async-start | bytes 917504 | tf_op jit(solution)/shard_map/all_to_all | solution.py:146
  66.8 19.4 %copy-start.3 = (s32[32]{0:T(128)S(1)}, s32[32]{0:T(128)}, u32[]{:S(2)}) copy-start(s32[32]{0:T(128)} %copy-done.2) | copy-start | bytes 388
  81.4 19.7 %all-to-all-start.1 = ((bf16[16,4,3584]{2,1,0:T(4,128)(2,1)}), bf16[16,4,3584]{2,1,0:T(4,128)(2,1)S(1)}, u32[]{:S(2)}, u32[]{:S(2)}) async-start(bf16[16,4,3584]{2,1,0:T(4,128)(2,1)} %reshape.133), calls=%async_computation.1 | async-start | bytes 917504 | tf_op jit(solution)/shard_map/all_to_all | solution.py:135
  89.1 22.2 %copy-start.6 = (u32[32]{0:T(128)S(1)}, u32[32]{0:T(128)}, u32[]{:S(2)}) copy-start(u32[32]{0:T(128)} %constant.148) | copy-start | bytes 388
  101.1 77.6 %all-to-all-start.3 = ((bf16[16,4,3584]{2,1,0:T(4,128)(2,1)}), bf16[16,4,3584]{2,1,0:T(4,128)(2,1)S(1)}, u32[]{:S(2)}, u32[]{:S(2)}) async-start(bf16[16,4,3584]{2,1,0:T(4,128)(2,1)} %reshape.138), calls=%async_computation.3 | async-start | bytes 917504 | tf_op jit(solution)/shard_map/all_to_all | solution.py:135
Sparse Core Ops, SparseCore 0:
  47.5 129.3 all-reduce.3
where the time goes:
time: 192 us; the launch traced here: 191 us
  waiting for transfers between devices  79.8 us (42%)
  between operations  29 us (15%)
  starting transfers between devices  28.4 us (15%)
  matrix products  17.5 us (9%)
  local copies, waits for them, and re-layouts  17.1 us (9%)
  other arithmetic  9.87 us (5%)
  blocking collectives  9.41 us (5%)
    psum x1, waiting for transfers between devices, spread(): return lax.psum(kept, axis)  64.3 us
    all_to_all x2, starting transfers between devices, shards(): lax.all_to_all(buffers[number], 'ep', split_axis=0, concat_axis=0, tiled=...  19.9 us
    dot_general x2, matrix products, expert_math(): jnp.dot(hidden_units, w_down[0], preferred_element_type=jnp.float32)  9.3 us
    all_to_all x2, waiting for transfers between devices, shards(): lax.all_to_all(buffers[number], 'ep', split_axis=0, concat_axis=0, tiled=...  9 us
    all_to_all x2, starting transfers between devices, expert_apart(): lax.all_to_all(expert_math(received), 'ep', split_axis=0, concat_axis=0,...  8.47 us
    all_to_all x2, waiting for transfers between devices, expert_apart(): lax.all_to_all(expert_math(received), 'ep', split_axis=0, concat_axis=0,...  6.46 us
    dot_general x2, matrix products, expert_math(): jnp.dot(flat_rows, w_gate[0], preferred_element_type=jnp.float32)  5.57 us
  transfers between devices with their start and end apart: 5, of which 3 were waited for; matrix products, arithmetic and copies ran while one was open for 20% of the time, Pallas kernels for 0%

commit v1 on v0

--- a/solution.py
+++ b/solution.py
@@ -10,7 +10,7 @@
 
 def spread(value, axis, source):
     kept = jnp.where(lax.axis_index(axis) == source, value, 0).astype(value.dtype)
-    return lax.psum(kept, axis)
+    return jnp.sum(lax.all_gather(kept, axis), axis=0)
 
 
 def attend(query_rows, cache_rows, fresh_rows, length, softmax_scale):

time: 192 us -> 363 us (1.89)
  waiting for transfers between devices: 79.8 us -> 238 us
  other arithmetic: 9.87 us -> 20.4 us
  starting transfers between devices: 28.4 us -> 34.3 us
  local copies, waits for them, and re-layouts: 17.1 us -> 12.7 us
    all_gather x0 -> x4, waiting for transfers between devices: none -> 198 us  [spread(): return jnp.sum(lax.all_gather(kept, axis), axis=0)]
    psum x1 -> x0, waiting for transfers between devices: 64.3 us -> none  [spread(): return lax.psum(kept, axis)]
    all_to_all x2, waiting for transfers between devices: 9 us -> 26.4 us  [shards(): lax.all_to_all(buffers[number], 'ep', split_axis=0, concat_axis=0, tiled=...]
    reduce_sum x0 -> x4, other arithmetic: none -> 11.4 us  [spread(): return jnp.sum(lax.all_gather(kept, axis), axis=0)]
    all_to_all x2, waiting for transfers between devices: 6.46 us -> 12.9 us  [expert_apart(): lax.all_to_all(expert_math(received), 'ep', split_axis=0, concat_axis=0,...]
    all_to_all x2, starting transfers between devices: 8.47 us -> 14.5 us  [expert_apart(): lax.all_to_all(expert_math(received), 'ep', split_axis=0, concat_axis=0,...]
  transfers between devices with their start and end apart: 5 -> 8, of which waited for: 3 -> 7; matrix products, arithmetic and copies ran while one was open for 20% -> 11% of each run, Pallas kernels for 0% -> 0%
where the time goes in v1:
time: 363 us; the launch traced here: 362 us
  waiting for transfers between devices  238 us (66%)
  starting transfers between devices  34.3 us (9%)
  between operations  28.5 us (8%)
  other arithmetic  20.4 us (6%)
  matrix products  18 us (5%)
  local copies, waits for them, and re-layouts  12.7 us (3%)
  blocking collectives  9.61 us (3%)
    all_gather x4, waiting for transfers between devices, spread(): return jnp.sum(lax.all_gather(kept, axis), axis=0)  198 us
    all_to_all x2, waiting for transfers between devices, shards(): lax.all_to_all(buffers[number], 'ep', split_axis=0, concat_axis=0, tiled=...  26.4 us
    all_to_all x2, starting transfers between devices, shards(): lax.all_to_all(buffers[number], 'ep', split_axis=0, concat_axis=0, tiled=...  19.7 us
    all_to_all x2, starting transfers between devices, expert_apart(): lax.all_to_all(expert_math(received), 'ep', split_axis=0, concat_axis=0,...  14.5 us
    all_to_all x2, waiting for transfers between devices, expert_apart(): lax.all_to_all(expert_math(received), 'ep', split_axis=0, concat_axis=0,...  12.9 us
    reduce_sum x4, other arithmetic, spread(): return jnp.sum(lax.all_gather(kept, axis), axis=0)  11.4 us
    dot_general x2, matrix products, expert_math(): jnp.dot(hidden_units, w_down[0], preferred_element_type=jnp.float32)  9.23 us
  transfers between devices with their start and end apart: 8, of which 7 were waited for; matrix products, arithmetic and copies ran while one was open for 11% of the time, Pallas kernels for 0%

profile of v1, /device:TPU:0, one launch (start us, length us, event | category | flops | bytes accessed | tf_op | source)
XLA Modules:
  0.0 362.1 jit_solution(3680410777547884569)
XLA Ops:
  7.2 1.3 constant_dynamic-slice_fusion.2
  9.2 1.3 fusion.82
  11.2 0.9 while.40
  24.0 0.8 while.42
  30.4 2.0 all-gather
  32.9 1.8 all-gather.1
  35.3 0.9 reshape.225
  36.2 12.6 %all-to-all-start = ((bf16[16,4,3584]{2,1,0:T(4,128)(2,1)}), bf16[16,4,3584]{2,1,0:T(4,128)(2,1)S(1)}, u32[]{:S(2)}, u32[]{:S(2)}) async-start(bf16[16,4,3584]{2,1,0:T(4,128)(2,1)} %reshape.225), calls=%async_computation | async-start | bytes 917504 | tf_op jit(solution)/shard_map/all_to_all | solution.py:146
  48.8 1.8 all-gather.2
  51.5 0.9 reshape.230
  52.4 17.4 %all-to-all-done = bf16[16,4,3584]{2,1,0:T(4,128)(2,1)S(1)} async-done(((bf16[16,4,3584]{2,1,0:T(4,128)(2,1)}), bf16[16,4,3584]{2,1,0:T(4,128)(2,1)S(1)}, u32[]{:S(2)}, u32[]{:S(2)}) %all-to-all-start) | async-done | bytes 458784 | tf_op jit(solution)/shard_map/all_to_all | solution.py:146
  69.8 7.1 %all-to-all-start.2 = ((bf16[16,4,3584]{2,1,0:T(4,128)(2,1)}), bf16[16,4,3584]{2,1,0:T(4,128)(2,1)S(1)}, u32[]{:S(2)}, u32[]{:S(2)}) async-start(bf16[16,4,3584]{2,1,0:T(4,128)(2,1)} %reshape.230), calls=%async_computation.2 | async-start | bytes 917504 | tf_op jit(solution)/shard_map/all_to_all | solution.py:146
  77.2 3.3 fusion.24
  80.5 4.6 %convolution_convert_fusion.1 = bf16[64,3584]{1,0:T(8,128)(2,1)S(1)} fusion(bf16[1,512,3584]{2,1,0:T(8,128)(2,1)} %param.31, bf16[64,3584]{1,0:T(8,128)(2,1)S(1)} %reshape.226, bf16[1,3584,512]{2,1,0:T(8,128)(2,1)} %param.30, f32[64,512]{1,0:T(8,128)S(1)} %fusion.24), kind=kOutput, calls=%fused_computation.25 | convolution fusion | flops 470188032 | bytes 8388608 | tf_op jit(solution)/shard_map/dot_general | solution.py:129
  85.1 0.9 reshape.227
  86.0 9.0 %all-to-all-done.2 = bf16[16,4,3584]{2,1,0:T(4,128)(2,1)S(1)} async-done(((bf16[16,4,3584]{2,1,0:T(4,128)(2,1)}), bf16[16,4,3584]{2,1,0:T(4,128)(2,1)S(1)}, u32[]{:S(2)}, u32[]{:S(2)}) %all-to-all-start.2) | async-done | bytes 458784 | tf_op jit(solution)/shard_map/all_to_all | solution.py:146
  95.0 9.3 %all-to-all-start.1 = ((bf16[16,4,3584]{2,1,0:T(4,128)(2,1)}), bf16[16,4,3584]{2,1,0:T(4,128)(2,1)S(1)}, u32[]{:S(2)}, u32[]{:S(2)}) async-start(bf16[16,4,3584]{2,1,0:T(4,128)(2,1)} %reshape.227), calls=%async_computation.1 | async-start | bytes 917504 | tf_op jit(solution)/shard_map/all_to_all | solution.py:135
  110.8 2.8 fusion.22
  113.5 4.6 %convolution_convert_fusion = bf16[64,3584]{1,0:T(8,128)(2,1)S(1)} fusion(bf16[1,512,3584]{2,1,0:T(8,128)(2,1)} %param.31, bf16[64,3584]{1,0:T(8,128)(2,1)S(1)} %reshape.231, bf16[1,3584,512]{2,1,0:T(8,128)(2,1)} %param.30, f32[64,512]{1,0:T(8,128)S(1)} %fusion.22), kind=kOutput, calls=%fused_computation.24 | convolution fusion | flops 470188032 | bytes 8388608 | tf_op jit(solution)/shard_map/dot_general | solution.py:129
  118.2 0.9 reshape.232
  119.0 1.7 all-to-all-done.1
  120.8 5.2 %all-to-all-start.3 = ((bf16[16,4,3584]{2,1,0:T(4,128)(2,1)}), bf16[16,4,3584]{2,1,0:T(4,128)(2,1)S(1)}, u32[]{:S(2)}, u32[]{:S(2)}) async-start(bf16[16,4,3584]{2,1,0:T(4,128)(2,1)} %reshape.232), calls=%async_computation.3 | async-start | bytes 917504 | tf_op jit(solution)/shard_map/all_to_all | solution.py:135
  128.3 11.2 %all-to-all-done.3 = bf16[16,4,3584]{2,1,0:T(4,128)(2,1)S(1)} async-done(((bf16[16,4,3584]{2,1,0:T(4,128)(2,1)}), bf16[16,4,3584]{2,1,0:T(4,128)(2,1)S(1)}, u32[]{:S(2)}, u32[]{:S(2)}) %all-to-all-start.3) | async-done | bytes 458784 | tf_op jit(solution)/shard_map/all_to_all | solution.py:135
  140.8 4.0 %all-reduce = bf16[2,4,3584]{2,1,0:T(4,128)(2,1)S(1)} all-reduce(f32[2,4,3584]{2,1,0:T(4,128)S(1)} %pad_maximum_fusion), channel_id=5, replica_groups=mesh['dp'=2,'ep'=16] {'dp'}, use_global_device_ids=true, to_apply=%region_31.33.clone | all-reduce | flops 28672 | bytes 172032
  145.4 2.9 reduce_sum.141
  148.3 49.7 %all-gather.8.cloned.1.call-done = bf16[16,2,128,512]{3,2,1,0:T(8,128)(2,1)} async-done(((bf16[1,2,128,512]{3,2,1,0:T(8,128)(2,1)}), bf16[16,2,128,512]{3,2,1,0:T(8,128)(2,1)}) %all-gather.8.cloned.1.call-update) | async-done | bytes 4194320 | tf_op jit(solution)/shard_map/all_gather | solution.py:13
  198.0 2.9 reduce_sum.139
  200.9 74.1 %all-gather.14.cloned.1.call-done = bf16[16,2,128,512]{3,2,1,0:T(8,128)(2,1)} async-done(((bf16[1,2,128,512]{3,2,1,0:T(8,128)(2,1)}), bf16[16,2,128,512]{3,2,1,0:T(8,128)(2,1)}) %all-gather.14.cloned.1.call-update) | async-done | bytes 4194320 | tf_op jit(solution)/shard_map/all_gather | solution.py:13
  275.0 2.9 reduce_sum.147
  277.9 73.9 %all-gather.12.cloned.1.call-done = bf16[16,2,128,512]{3,2,1,0:T(8,128)(2,1)} async-done(((bf16[1,2,128,512]{3,2,1,0:T(8,128)(2,1)}), bf16[16,2,128,512]{3,2,1,0:T(8,128)(2,1)}) %all-gather.12.cloned.1.call-update) | async-done | bytes 4194320 | tf_op jit(solution)/shard_map/all_gather | solution.py:13
  351.8 2.9 reduce_sum.145
  354.8 0.8 maximum_bitcast_fusion
  (113 shorter events, 19.3 us)
Async XLA Ops:
  7.2 3.7 %copy-start = (bf16[2,1,2,128,576]{3,4,2,1,0:T(8,128)(2,1)S(1)}, bf16[2,1,2,128,576]{3,4,2,1,0:T(8,128)(2,1)}, u32[]{:S(2)}) copy-start(bf16[2,1,2,128,576]{3,4,2,1,0:T(8,128)(2,1)} %param.24) | copy-start | bytes 1769476
  7.2 138.2 %all-gather.10.cloned.1.call-start = ((), (), s32[]{:S(2)}) async-start(), calls=%async_computation.5 | async-start | bytes 4456448 | tf_op jit(solution)/shard_map/all_gather | solution.py:13
  10.9 1.6 copy-start.2
  11.2 2.3 copy-start.4
  19.7 178.3 %all-gather.8.cloned.1.call-start = ((), (), s32[]{:S(2)}) async-start(), calls=%async_computation.4 | async-start | bytes 4456448 | tf_op jit(solution)/shard_map/all_gather | solution.py:13
  20.5 254.5 %all-gather.14.cloned.1.call-start = ((), (), s32[]{:S(2)}) async-start(), calls=%async_computation.7 | async-start | bytes 4456448 | tf_op jit(solution)/shard_map/all_gather | solution.py:13
  28.0 2.4 copy-start.3
  28.0 4.9 %copy-start.1 = (bf16[2,1,2,3584]{3,2,1,0:T(2,128)(2,1)S(1)}, bf16[2,1,2,3584]{3,2,1,0:T(2,128)(2,1)}, u32[]{:S(2)}) copy-start(bf16[2,1,2,3584]{3,2,1,0:T(2,128)(2,1)} %param.26) | copy-start | bytes 86020
  28.0 8.2 %copy-start.5 = (bf16[2,1,2,8]{3,2,1,0:T(2,128)(2,1)S(1)}, bf16[2,1,2,8]{3,2,1,0:T(2,128)(2,1)}, u32[]{:S(2)}) copy-start(bf16[2,1,2,8]{3,2,1,0:T(2,128)(2,1)} %param.28) | copy-start | bytes 196
  29.8 322.0 %all-gather.12.cloned.1.call-start = ((), (), s32[]{:S(2)}) async-start(), calls=%async_computation.6 | async-start | bytes 4456448 | tf_op jit(solution)/shard_map/all_gather | solution.py:13
  36.2 33.6 %all-to-all-start = ((bf16[16,4,3584]{2,1,0:T(4,128)(2,1)}), bf16[16,4,3584]{2,1,0:T(4,128)(2,1)S(1)}, u32[]{:S(2)}, u32[]{:S(2)}) async-start(bf16[16,4,3584]{2,1,0:T(4,128)(2,1)} %reshape.225), calls=%async_computation | async-start | bytes 917504 | tf_op jit(solution)/shard_map/all_to_all | solution.py:146
  69.8 25.2 %all-to-all-start.2 = ((bf16[16,4,3584]{2,1,0:T(4,128)(2,1)}), bf16[16,4,3584]{2,1,0:T(4,128)(2,1)S(1)}, u32[]{:S(2)}, u32[]{:S(2)}) async-start(bf16[16,4,3584]{2,1,0:T(4,128)(2,1)} %reshape.230), calls=%async_computation.2 | async-start | bytes 917504 | tf_op jit(solution)/shard_map/all_to_all | solution.py:146
  95.0 25.7 %all-to-all-start.1 = ((bf16[16,4,3584]{2,1,0:T(4,128)(2,1)}), bf16[16,4,3584]{2,1,0:T(4,128)(2,1)S(1)}, u32[]{:S(2)}, u32[]{:S(2)}) async-start(bf16[16,4,3584]{2,1,0:T(4,128)(2,1)} %reshape.227), calls=%async_computation.1 | async-start | bytes 917504 | tf_op jit(solution)/shard_map/all_to_all | solution.py:135
  113.5 12.6 %copy-start.6 = (u32[32]{0:T(128)S(1)}, u32[32]{0:T(128)}, u32[]{:S(2)}) copy-start(u32[32]{0:T(128)} %constant.152) | copy-start | bytes 388
  120.8 18.7 %all-to-all-start.3 = ((bf16[16,4,3584]{2,1,0:T(4,128)(2,1)}), bf16[16,4,3584]{2,1,0:T(4,128)(2,1)S(1)}, u32[]{:S(2)}, u32[]{:S(2)}) async-start(bf16[16,4,3584]{2,1,0:T(4,128)(2,1)} %reshape.232), calls=%async_computation.3 | async-start | bytes 917504 | tf_op jit(solution)/shard_map/all_to_all | solution.py:135
Sparse Core Ops, SparseCore 0:
  19.8 99.3 all-gather.9
  121.9 76.0 all-gather.7
  200.8 74.1 all-gather.13
  277.6 74.1 all-gather.11
